TPU v7x, 256 devices: a whole 4x4x8 slice. The times are simulated.
256 devices in a mesh: context: 32 (over z, x_lo, core), tensor: 8 (over x_hi, y).
Axes of the slice: x: 4 (x_hi: 2, x_lo: 2; x = x_hi * 2 + x_lo), y: 4, z: 8, core: 2. Of those that a mesh axis runs over, the one named last changes fastest.
Arguments:
- activations: bfloat16 [6144, 5120], P(('context', 'tensor')), may hold values from -6 to 6
- queries: bfloat16 [6144, 5120], P('context', 'tensor'), may hold values from -44 to 44
- key_weight: bfloat16 [5120, 1024], P(None, 'tensor'), may hold values from -0.5 to 1.1
- value_projection_weight: bfloat16 [5120, 1024], P(None, 'tensor'), may hold values from -0.078125 to 0.078125
- output_gradient: bfloat16 [6144, 5120], P('context', 'tensor'), may hold values from -6 to 6
- span_order: int32 [64], replicated, may hold values from 0 to 63, as said below
- doc_ids: int32 [6144], replicated, may hold values from 0 to 4, as said below
Outputs:
- attended: bfloat16 [6144, 5120], P('context', 'tensor')
- grad_queries: bfloat16 [6144, 5120], P('context', 'tensor')
- grad_inputs: bfloat16 [6144, 5120], P(('context', 'tensor'))
- grad_key_weight: float32 [5120, 1024], P('context', 'tensor')
- grad_value_weight: float32 [5120, 1024], P('context', 'tensor')
Inputs may be any that keep to these rules, and one draw needn't show every extreme that they name: `span_order`: each number once. `doc_ids`: taken in order of positions, the document numbers never fall; one document holds exactly 3072 positions and none holds more.
All inputs are finite; a program needn't handle non-finite values.
Results may differ from a plain program's by a relative error of at most 0.02.
Values may be sent and summed in bfloat16 or wider, within the bound.
No kernel may reach another device: no remote copies, remote signals or barrier semaphores. Data moves between devices by JAX's collectives and lax.ppermute only.
A program may use at most 192 MiB of HBM per device.

v0:
```python
import math
import jax
import jax.numpy as jnp
from jax import lax
from jax.sharding import PartitionSpec as P

HEAD_SIZE = 128
SPAN = 96


def on_device(
    activations, queries, key_weight, value_projection_weight, output_gradient, span_order, doc_ids
):
    local_rows = lax.all_gather(activations, "tensor", axis=0, tiled=True)
    shard_len = local_rows.shape[0]
    seq_len = doc_ids.shape[0]
    head_dim = HEAD_SIZE
    kv_width = key_weight.shape[1]
    kv_heads = kv_width // head_dim
    heads_per_group = queries.shape[1] // kv_width
    inv_root = 1.0 / math.sqrt(head_dim)
    key_local = jnp.dot(local_rows, key_weight, preferred_element_type=jnp.float32).astype(
        jnp.bfloat16
    )
    value_local = jnp.dot(
        local_rows, value_projection_weight, preferred_element_type=jnp.float32
    ).astype(jnp.bfloat16)
    row_ids = jnp.arange(seq_len, dtype=jnp.int32)
    span_match = (row_ids // SPAN)[:, None] == jnp.arange(span_order.shape[0], dtype=jnp.int32)[
        None, :
    ]
    all_pos = jnp.sum(jnp.where(span_match, span_order[None, :], 0), axis=1) * SPAN + row_ids % SPAN
    first_row = lax.axis_index("context") * shard_len
    query_pos = lax.dynamic_slice_in_dim(all_pos, first_row, shard_len)
    query_doc = lax.dynamic_slice_in_dim(doc_ids, first_row, shard_len)
    query_heads = queries.reshape(shard_len, kv_heads, heads_per_group, head_dim)
    grad_heads = output_gradient.reshape(shard_len, kv_heads, heads_per_group, head_dim)

    def visible():
        pair_mask = (query_doc[:, None] == doc_ids[None, :]) & (
            all_pos[None, :] <= query_pos[:, None]
        )
        return pair_mask[:, None, None, :]

    def scores_of(key_heads_split):
        return (
            jnp.einsum(
                "sgjd,ngd->sgjn", query_heads, key_heads_split, preferred_element_type=jnp.float32
            )
            * inv_root
        )

    stats_shape = (shard_len, kv_heads, heads_per_group)
    run_max = jnp.full(stats_shape, -1e30, jnp.float32)
    key_piece = lax.all_gather(key_local, "context", axis=0, tiled=True)
    value_piece = lax.all_gather(value_local, "context", axis=0, tiled=True)
    piece_len = key_piece.shape[0]
    pair_mask = visible()
    scores = scores_of(key_piece.reshape(piece_len, kv_heads, head_dim))
    new_max = jnp.maximum(run_max, jnp.max(jnp.where(pair_mask, scores, -1e30), axis=3))
    weights = jnp.where(pair_mask, jnp.exp(scores - new_max[..., None]), 0.0)
    value_heads_split = value_piece.reshape(piece_len, kv_heads, head_dim)
    summed = jnp.einsum(
        "sgjn,ngd->sgjd",
        weights.astype(jnp.bfloat16),
        value_heads_split,
        preferred_element_type=jnp.float32,
    )
    final_sum = jnp.sum(weights, axis=3)
    attended_low = (summed / final_sum[..., None]).astype(jnp.bfloat16)
    log_totals = new_max + jnp.log(final_sum)
    row_delta = jnp.sum(grad_heads.astype(jnp.float32) * attended_low.astype(jnp.float32), axis=3)
    key_piece = lax.all_gather(key_local, "context", axis=0, tiled=True)
    value_piece = lax.all_gather(value_local, "context", axis=0, tiled=True)
    piece_len = key_piece.shape[0]
    score_piece_len = key_piece.shape[0]
    pair_mask = visible()
    key_heads_split = key_piece.reshape(score_piece_len, kv_heads, head_dim)
    value_heads_split = value_piece.reshape(score_piece_len, kv_heads, head_dim)
    scores = scores_of(key_heads_split)
    probs = jnp.where(pair_mask, jnp.exp(scores - log_totals[..., None]), 0.0)
    grad_probs = jnp.einsum(
        "sgjd,ngd->sgjn", grad_heads, value_heads_split, preferred_element_type=jnp.float32
    )
    grad_scores = (probs * (grad_probs - row_delta[..., None]) * inv_root).astype(jnp.bfloat16)
    probs, grad_scores, key_heads_split = (probs, grad_scores, key_heads_split)
    grad_v_part = jnp.einsum(
        "sgjn,sgjd->ngd", probs.astype(jnp.bfloat16), grad_heads, preferred_element_type=jnp.float32
    )
    grad_q = jnp.einsum(
        "sgjn,ngd->sgjd", grad_scores, key_heads_split, preferred_element_type=jnp.float32
    )
    grad_k_part = jnp.einsum(
        "sgjn,sgjd->ngd", grad_scores, query_heads, preferred_element_type=jnp.float32
    )
    grad_k_buf = grad_k_part.reshape(piece_len, kv_width)
    grad_v_buf = grad_v_part.reshape(piece_len, kv_width)
    grad_q, grad_k_buf, grad_v_buf = (grad_q, grad_k_buf, grad_v_buf)
    grad_k_own, grad_v_own = (
        lax.psum_scatter(
            grad_k_buf.astype(jnp.bfloat16), "context", scatter_dimension=0, tiled=True
        ).astype(jnp.float32),
        lax.psum_scatter(
            grad_v_buf.astype(jnp.bfloat16), "context", scatter_dimension=0, tiled=True
        ).astype(jnp.float32),
    )
    grad_k_low = grad_k_own.astype(jnp.bfloat16)
    grad_v_low = grad_v_own.astype(jnp.bfloat16)
    grad_inputs = lax.psum_scatter(
        (
            jnp.dot(grad_k_low, key_weight.T, preferred_element_type=jnp.float32)
            + jnp.dot(grad_v_low, value_projection_weight.T, preferred_element_type=jnp.float32)
        ).astype(jnp.bfloat16),
        "tensor",
        scatter_dimension=0,
        tiled=True,
    )
    grad_kv = jnp.concatenate([grad_k_low, grad_v_low], axis=1)
    partial_grads = lax.dot_general(
        local_rows, grad_kv, (((0,), (0,)), ((), ())), preferred_element_type=jnp.float32
    )
    weight_grads = lax.psum_scatter(
        partial_grads.astype(jnp.bfloat16), "context", scatter_dimension=0, tiled=True
    ).astype(jnp.float32)
    attended = attended_low.reshape(shard_len, heads_per_group * kv_width)
    grad_queries = grad_q.astype(jnp.bfloat16).reshape(shard_len, heads_per_group * kv_width)
    return (
        attended,
        grad_queries,
        grad_inputs,
        weight_grads[:, :kv_width],
        weight_grads[:, kv_width:],
    )


def solution(mesh):
    return jax.shard_map(
        on_device,
        mesh=mesh,
        in_specs=(
            P(("context", "tensor"), None),
            P("context", "tensor"),
            P(None, "tensor"),
            P(None, "tensor"),
            P("context", "tensor"),
            P(),
            P(),
        ),
        out_specs=(
            P("context", "tensor"),
            P("context", "tensor"),
            P(("context", "tensor"), None),
            P("context", "tensor"),
            P("context", "tensor"),
        ),
        check_vma=False,
    )
```

profile of v0, /device:TPU:32, one launch (start us, length us, event | category | flops | bytes accessed | tf_op | source)
XLA Modules:
  0.0 701.8 jit_solution(13686100925459275635)
XLA Ops:
  7.2 0.0 copy-start
  7.2 0.0 copy-start.5
  7.2 0.0 copy-start.9
  7.2 0.0 copy-start.8
  7.2 0.0 all-gather.4.cloned.1.call-start
  7.3 0.7 all-gather.4.cloned.1.call-update
  7.9 0.0 all-gather.8.cloned.1.call-start
  8.0 62.8 %all-gather.4.cloned.1.call-done = bf16[192,5120]{1,0:T(8,128)(2,1)} async-done(((bf16[24,5120]{1,0:T(8,128)(2,1)}), bf16[192,5120]{1,0:T(8,128)(2,1)}) %all-gather.4.cloned.1.call-update) | async-done | bytes 1966096 | tf_op jit(solution)/shard_map/all_gather | solution.py:14
  70.8 0.0 copy-done
  70.8 0.0 copy-start.1
  70.8 3.0 convolution_convert_fusion.1
  73.8 0.0 all-gather.8.cloned.1.call-update
  73.8 0.0 all-gather.6.cloned.1.call-start
  73.9 2.0 copy.51
  75.8 0.0 copy-done.5
  75.8 0.9 copy.49
  76.7 2.1 copy.52
  78.9 0.0 copy-done.9
  78.9 0.3 select_reduce_fusion
  79.2 0.1 dynamic_slice.7
  79.3 0.0 copy-done.8
  79.3 0.1 dynamic_slice.6
  79.4 1.8 copy.46
  81.2 2.0 compare_and_fusion
  83.2 0.0 copy-done.1
  83.2 2.6 convolution_convert_fusion.2
  85.9 0.0 all-gather.6.cloned.1.call-update
  85.9 0.0 reduce-scatter.7.cloned.1.call-start
  85.9 49.3 %all-gather.8.cloned.1.call-done = bf16[6144,128]{1,0:T(8,128)(2,1)} async-done(((bf16[192,128]{1,0:T(8,128)(2,1)}), bf16[6144,128]{1,0:T(8,128)(2,1)}) %all-gather.8.cloned.1.call-update) | async-done | bytes 1572880 | tf_op jit(solution)/shard_map/all_gather | solution.py:55
  135.3 11.6 %fusion.2 = (f32[192,5]{0,1:T(8,128)S(1)}, f32[6144,192,5]{0,1,2:T(8,128)}) fusion(pred[192,6144]{1,0:T(8,128)(4,1)} %compare_and_fusion, bf16[192,5,128]{0,2,1:T(8,128)(2,1)} %bitcast.161, bf16[6144,128]{1,0:T(8,128)(2,1)} %all-gather.8.cloned.1.call-done), kind=kOutput, calls=%fused_computation.7 | convolution fusion | flops 1527643136 | bytes 26595072 | tf_op jit(solution)/shard_map/sgjd,ngd->sgjn/dot_general | solution.py:47
  146.8 0.0 copy-done.3
  146.9 11.4 %fusion.8 = f32[192,5]{0,1:T(8,128)S(1)} fusion(f32[6144,192,5]{0,1,2:T(8,128)} %get-tuple-element.28, f32[192,5]{0,1:T(8,128)S(1)} %broadcast_maximum_fusion, pred[192,6144]{1,0:T(8,128)(4,1)S(1)} %copy-done.3), kind=kLoop, calls=%fused_computation.13 | loop fusion | flops 23592000 | bytes 24780288 | tf_op jit(solution)/shard_map/reduce_sum | solution.py:69
  158.3 43.2 %all-gather.6.cloned.1.call-done = bf16[6144,128]{1,0:T(8,128)(2,1)} async-done(((bf16[192,128]{1,0:T(8,128)(2,1)}), bf16[6144,128]{1,0:T(8,128)(2,1)}) %all-gather.6.cloned.1.call-update) | async-done | bytes 1572880 | tf_op jit(solution)/shard_map/all_gather | solution.py:56
  201.5 13.0 %multiply_reduce_fusion = (f32[192,5]{0,1:T(8,128)S(1)}, bf16[192,1,5,128]{3,0,2,1:T(8,128)(2,1)S(1)}) fusion(f32[192,1,5,128]{3,0,2,1:T(8,128)} %copy.52, f32[192,5]{0,1:T(8,128)S(1)} %fusion.8, f32[6144,192,5]{0,1,2:T(8,128)} %get-tuple-element.28, f32[192,5]{0,1:T(8,128)S(1)} %broadcast_maximum_fusion, pred[192,6144]{1,0:T(8,128)(4,1)} %compare_and_fusion, ...), kind=kOutput, calls=%fused_computation.49 | convolution fusion | flops 1534155776 | bytes 27094272 | tf_op jit(solution)/shard_map/sgjn,ngd->sgjd/dot_general | solution.py:63
  214.5 19.3 %fusion.1 = bf16[192,1,5,6144]{3,0,2,1:T(8,128)(2,1)} fusion(f32[6144,192,5]{0,1,2:T(8,128)} %get-tuple-element.28, bf16[192,5,128]{0,2,1:T(8,128)(2,1)} %bitcast.159, f32[192,5]{0,1:T(8,128)S(1)} %get-tuple-element.29, f32[192,5]{0,1:T(8,128)S(1)} %log_add_fusion, pred[192,6144]{1,0:T(8,128)(4,1)} %compare_and_fusion, ...), kind=kOutput, calls=%fused_computation.2 | convolution fusion | flops 1551237120 | bytes 38395392 | tf_op jit(solution)/shard_map/sgjd,ngd->sgjn/dot_general | solution.py:82
  233.8 9.9 %fusion.31 = bf16[6144,128]{1,0:T(8,128)(2,1)} fusion(bf16[192,5,128]{0,2,1:T(8,128)(2,1)} %bitcast.162, bf16[192,1,5,6144]{3,0,2,1:T(8,128)(2,1)} %fusion.1), kind=kOutput, calls=%fused_computation.28 | convolution fusion | flops 1510735872 | bytes 13615104 | tf_op jit(solution)/shard_map/sgjn,sgjd->ngd/dot_general | solution.py:93
  243.7 0.0 reduce-scatter.7.cloned.1.call-update
  243.7 0.0 reduce-scatter.9.cloned.1.call-start
  243.8 12.6 %fusion.28 = bf16[6144,128]{1,0:T(8,128)(2,1)} fusion(bf16[192,5,128]{0,2,1:T(8,128)(2,1)} %bitcast.160, f32[6144,192,5]{0,1,2:T(8,128)} %get-tuple-element.28, f32[192,5]{0,1:T(8,128)S(1)} %log_add_fusion, pred[192,6144]{1,0:T(8,128)(4,1)} %compare_and_fusion), kind=kOutput, calls=%fused_computation.27 | convolution fusion | flops 1534328832 | bytes 26595072 | tf_op jit(solution)/shard_map/sgjn,sgjd->ngd/dot_general | solution.py:87
  256.4 0.0 reduce-scatter.9.cloned.1.call-update
  256.4 0.0 reduce-scatter.13.cloned.1.call-start
  256.4 100.9 %reduce-scatter.7.cloned.1.call-done = bf16[192,128]{1,0:T(8,128)(2,1)} async-done(((bf16[6144,128]{1,0:T(8,128)(2,1)}), bf16[192,128]{1,0:T(8,128)(2,1)}) %reduce-scatter.7.cloned.1.call-update) | async-done | bytes 49168 | tf_op jit(solution)/shard_map/reduce_scatter | solution.py:100
  357.4 120.2 %reduce-scatter.9.cloned.1.call-done = bf16[192,128]{1,0:T(8,128)(2,1)} async-done(((bf16[6144,128]{1,0:T(8,128)(2,1)}), bf16[192,128]{1,0:T(8,128)(2,1)}) %reduce-scatter.9.cloned.1.call-update) | async-done | bytes 49168 | tf_op jit(solution)/shard_map/reduce_scatter | solution.py:103
  477.6 3.2 fusion.35
  480.8 4.4 copy.64
  485.2 0.0 reduce-scatter.13.cloned.1.call-update
  485.3 0.0 reduce-scatter.11.cloned.1.call-start
  485.3 0.0 copy-done.6
  485.3 0.7 fusion.88
  486.0 0.6 copy-done.2
  486.5 0.0 copy-done.7
  486.5 2.0 fusion.34
  488.5 0.0 reduce-scatter.11.cloned.1.call-update
  488.6 0.2 copy.48
  488.8 0.9 copy.56
  489.6 0.4 copy-done.4
  490.0 6.1 fusion.51
  496.2 0.2 copy.53
  496.3 0.9 copy.57
  497.2 107.8 %reduce-scatter.13.cloned.1.call-done = bf16[160,256]{1,0:T(8,128)(2,1)} async-done(((bf16[5120,256]{1,0:T(8,128)(2,1)}), bf16[160,256]{1,0:T(8,128)(2,1)}) %reduce-scatter.13.cloned.1.call-update) | async-done | bytes 81936
  605.0 1.0 copy.65
  606.1 0.7 copy.58
  606.8 0.7 copy.59
  607.5 87.4 %reduce-scatter.11.cloned.1.call-done = bf16[24,5120]{1,0:T(8,128)(2,1)} async-done(((bf16[192,5120]{1,0:T(8,128)(2,1)}), bf16[24,5120]{1,0:T(8,128)(2,1)}) %reduce-scatter.11.cloned.1.call-update) | async-done | bytes 245776 | tf_op jit(solution)/shard_map/reduce_scatter | solution.py:109
  (10 shorter events, 0.1 us)
Async XLA Ops:
  7.2 63.6 %copy-start = (bf16[5120,128]{1,0:T(8,128)(2,1)S(1)}, bf16[5120,128]{1,0:T(8,128)(2,1)}, u32[]{:S(2)}) copy-start(bf16[5120,128]{1,0:T(8,128)(2,1)} %param.9) | copy-start | bytes 3932164
  7.2 68.6 %copy-start.5 = (bf16[192,640]{1,0:T(8,128)(2,1)S(1)}, bf16[192,640]{1,0:T(8,128)(2,1)}, u32[]{:S(2)}) copy-start(bf16[192,640]{1,0:T(8,128)(2,1)} %param.11) | copy-start | bytes 737284
  7.2 71.7 %copy-start.9 = (s32[64]{0:T(128)S(1)}, s32[64]{0:T(128)}, u32[]{:S(2)}) copy-start(s32[64]{0:T(128)} %param.12) | copy-start | bytes 772
  7.2 72.1 %copy-start.8 = (s32[6144]{0:T(1024)S(1)}, s32[6144]{0:T(1024)}, u32[]{:S(2)}) copy-start(s32[6144]{0:T(1024)} %param.13) | copy-start | bytes 73732
  7.2 63.6 %all-gather.4.cloned.1.call-start = ((), (), s32[]{:S(2)}) async-start(), calls=%async_computation.4 | async-start | bytes 2211840 | tf_op jit(solution)/shard_map/all_gather | solution.py:14
  7.9 127.3 %all-gather.8.cloned.1.call-start = ((), (), s32[]{:S(2)}) async-start(), calls=%async_computation.6 | async-start | bytes 1622016 | tf_op jit(solution)/shard_map/all_gather | solution.py:55
  70.8 12.4 %copy-start.1 = (bf16[192,5120]{1,0:T(8,128)(2,1)S(1)}, bf16[192,5120]{1,0:T(8,128)(2,1)}, u32[]{:S(2)}) copy-start(bf16[192,5120]{1,0:T(8,128)(2,1)} %all-gather.4.cloned.1.call-done) | copy-start | bytes 5898244
  73.8 127.7 %all-gather.6.cloned.1.call-start = ((), (), s32[]{:S(2)}) async-start(), calls=%async_computation.5 | async-start | bytes 1622016 | tf_op jit(solution)/shard_map/all_gather | solution.py:56
  85.9 271.5 %reduce-scatter.7.cloned.1.call-start = ((), (), s32[]{:S(2)}) async-start(), calls=%async_computation.7 | async-start | bytes 1622016 | tf_op jit(solution)/shard_map/reduce_scatter | solution.py:100
  135.3 11.6 %copy-start.3 = (pred[192,6144]{1,0:T(8,128)(4,1)S(1)}, pred[192,6144]{1,0:T(8,128)(4,1)}, u32[]{:S(2)}) copy-start(pred[192,6144]{1,0:T(8,128)(4,1)} %compare_and_fusion) | copy-start | bytes 3538948
  243.7 233.9 %reduce-scatter.9.cloned.1.call-start = ((), (), s32[]{:S(2)}) async-start(), calls=%async_computation.8 | async-start | bytes 1622016 | tf_op jit(solution)/shard_map/reduce_scatter | solution.py:103
  256.4 348.7 %reduce-scatter.13.cloned.1.call-start = ((), (), s32[]{:S(2)}) async-start(), calls=%async_computation.10 | async-start | bytes 2703360
  480.8 4.5 copy-start.6
  485.2 1.3 copy-start.2
  485.2 1.3 copy-start.7
  485.3 209.7 %reduce-scatter.11.cloned.1.call-start = ((), (), s32[]{:S(2)}) async-start(), calls=%async_computation.9 | async-start | bytes 2211840 | tf_op jit(solution)/shard_map/reduce_scatter | solution.py:109
  488.5 1.5 copy-start.4
Sparse Core Ops, SparseCore 0:
  10.6 60.1 all-gather.3
  73.9 61.2 all-gather.7
  137.7 63.7 all-gather.5
  243.9 113.4 reduce-scatter.6
  359.7 117.8 reduce-scatter.8
  485.4 119.6 reduce-scatter.12
  609.6 85.2 reduce-scatter.10
where the time goes:
time: 702 us
  waiting for transfers between devices  573 us (82%)
  matrix products  83.9 us (12%)
  local copies, waits for them, and re-layouts  16.9 us (2%)
  between operations  14.3 us (2%)
  other arithmetic  13.8 us (2%)
    reduce_scatter x1, waiting for transfers between devices, on_device(): lax.psum_scatter(grad_v_buf.astype(jnp.bfloat16), 'context', scatter_dime...  120 us
    unnamed x8, waiting for transfers between devices  109 us
    reduce_scatter x1, waiting for transfers between devices, on_device(): lax.psum_scatter(grad_k_buf.astype(jnp.bfloat16), 'context', scatter_dime...  101 us
    reduce_scatter x1, waiting for transfers between devices, on_device(): lax.psum_scatter((jnp.dot(grad_k_low, key_weight.T, preferred_element_typ...  87.4 us
    all_gather x1, waiting for transfers between devices, on_device(): local_rows = lax.all_gather(activations, 'tensor', axis=0, tiled=True)  62.8 us
    all_gather x1, waiting for transfers between devices, on_device(): key_piece = lax.all_gather(key_local, 'context', axis=0, tiled=True)  49.3 us
    all_gather x1, waiting for transfers between devices, on_device(): value_piece = lax.all_gather(value_local, 'context', axis=0, tiled=True)  43.2 us
    dot_general x1, matrix products, on_device(): jnp.einsum('sgjd,ngd->sgjn', grad_heads, value_heads_split, preferred_ele...  19.3 us
  transfers between devices with their start and end apart: 7, of which 7 were waited for; matrix products, arithmetic and copies ran while one was open for 9% of the time, Pallas kernels for 0%

commit v1 on v0

--- a/solution.py
+++ b/solution.py
@@ -3,6 +3,7 @@
 import jax.numpy as jnp
 from jax import lax
 from jax.sharding import PartitionSpec as P
+from jax.lax import all_gather
 
 HEAD_SIZE = 128
 SPAN = 96
@@ -52,8 +53,12 @@
 
     stats_shape = (shard_len, kv_heads, heads_per_group)
     run_max = jnp.full(stats_shape, -1e30, jnp.float32)
-    key_piece = lax.all_gather(key_local, "context", axis=0, tiled=True)
-    value_piece = lax.all_gather(value_local, "context", axis=0, tiled=True)
+    supply_edges = lambda piece_in, tile_in: jnp.split(
+        all_gather(jnp.concatenate([piece_in, tile_in], axis=1), "context", axis=0, tiled=True),
+        [piece_in.shape[1]],
+        axis=1,
+    )
+    key_piece, value_piece = supply_edges(key_local, value_local)
     piece_len = key_piece.shape[0]
     pair_mask = visible()
     scores = scores_of(key_piece.reshape(piece_len, kv_heads, head_dim))

time: 702 us -> 753 us (1.073)
  waiting for transfers between devices: 573 us -> 618 us
  matrix products: 83.9 us -> 94.1 us
    all_gather x0 -> x1, waiting for transfers between devices: none -> 55.4 us  [on_device(): all_gather(jnp.concatenate([piece_in, tile_in], axis=1), 'context', axis=...]
    all_gather x1, waiting for transfers between devices: 43.2 us -> 28.9 us  [on_device(): value_piece = lax.all_gather(value_local, 'context', axis=0, tiled=True)]
    dot_general x1 -> x2, matrix products: 11.6 us -> 23.6 us  [scores_of(): jnp.einsum('sgjd,ngd->sgjn', query_heads, key_heads_split, preferred_elem...]
    unnamed x8 -> x9, waiting for transfers between devices: 109 us -> 108 us
  transfers between devices with their start and end apart: 7 -> 8, of which waited for: 7 -> 8; matrix products, arithmetic and copies ran while one was open for 9% -> 11% of each run, Pallas kernels for 0% -> 0%
where the time goes in v1:
time: 753 us
  waiting for transfers between devices  618 us (82%)
  matrix products  94.1 us (12%)
  other arithmetic  14.8 us (2%)
  between operations  14.3 us (2%)
  local copies, waits for them, and re-layouts  11.3 us (2%)
    reduce_scatter x1, waiting for transfers between devices, on_device(): lax.psum_scatter(grad_v_buf.astype(jnp.bfloat16), 'context', scatter_dime...  120 us
    unnamed x9, waiting for transfers between devices  108 us
    reduce_scatter x1, waiting for transfers between devices, on_device(): lax.psum_scatter(grad_k_buf.astype(jnp.bfloat16), 'context', scatter_dime...  101 us
    reduce_scatter x1, waiting for transfers between devices, on_device(): lax.psum_scatter((jnp.dot(grad_k_low, key_weight.T, preferred_element_typ...  87.5 us
    all_gather x1, waiting for transfers between devices, on_device(): local_rows = lax.all_gather(activations, 'tensor', axis=0, tiled=True)  62.8 us
    all_gather x1, waiting for transfers between devices, on_device(): all_gather(jnp.concatenate([piece_in, tile_in], axis=1), 'context', axis=...  55.4 us
    all_gather x1, waiting for transfers between devices, on_device(): key_piece = lax.all_gather(key_local, 'context', axis=0, tiled=True)  53.9 us
    all_gather x1, waiting for transfers between devices, on_device(): value_piece = lax.all_gather(value_local, 'context', axis=0, tiled=True)  28.9 us
  transfers between devices with their start and end apart: 8, of which 8 were waited for; matrix products, arithmetic and copies ran while one was open for 11% of the time, Pallas kernels for 0%

profile of v1, /device:TPU:32, one launch (start us, length us, event | category | flops | bytes accessed | tf_op | source)
XLA Modules:
  0.0 752.8 jit_solution(8677446344581257144)
XLA Ops:
  7.2 0.0 copy-start
  7.2 0.0 all-gather.5.cloned.1.call-start
  7.2 0.7 all-gather.5.cloned.1.call-update
  7.9 0.0 all-gather.9.cloned.1.call-start
  8.0 62.8 %all-gather.5.cloned.1.call-done = bf16[192,5120]{1,0:T(8,128)(2,1)} async-done(((bf16[24,5120]{1,0:T(8,128)(2,1)}), bf16[192,5120]{1,0:T(8,128)(2,1)}) %all-gather.5.cloned.1.call-update) | async-done | bytes 1966096 | tf_op jit(solution)/shard_map/all_gather | solution.py:15
  70.8 0.0 copy-done
  70.8 2.8 convolution_convert_fusion.2
  73.6 0.0 all-gather.9.cloned.1.call-update
  73.6 0.0 all-gather.7.cloned.1.call-start
  73.7 2.6 convolution_convert_fusion.1
  76.3 0.0 copy-start.5
  76.4 1.5 pad_maximum_fusion
  77.8 0.0 all-gather.7.cloned.1.call-update
  77.8 0.0 all-gather.11.cloned.1.call-start
  77.9 0.2 copy.55
  78.1 0.9 copy.53
  79.0 0.2 copy.56
  79.3 0.3 select_reduce_fusion
  79.6 0.1 dynamic_slice.7
  79.7 0.0 copy-done.11
  79.7 0.1 dynamic_slice.6
  79.8 0.0 copy-done.6
  79.8 0.2 copy.49
  80.0 1.0 compare_and_fusion
  81.0 0.0 all-gather.11.cloned.1.call-update
  81.0 0.2 reduce-scatter.7.cloned.1.call-start
  81.2 53.9 %all-gather.9.cloned.1.call-done = bf16[6144,128]{1,0:T(8,128)(2,1)} async-done(((bf16[192,128]{1,0:T(8,128)(2,1)}), bf16[6144,128]{1,0:T(8,128)(2,1)}) %all-gather.9.cloned.1.call-update) | async-done | bytes 1572880 | tf_op jit(solution)/shard_map/all_gather | solution.py:78
  135.1 12.5 %fusion.38 = f32[6144,192,5]{0,1,2:T(8,128)} fusion(bf16[192,5,128]{0,2,1:T(8,128)(2,1)S(1)} %bitcast.176, bf16[6144,128]{1,0:T(8,128)(2,1)} %all-gather.9.cloned.1.call-done), kind=kOutput, calls=%fused_computation.39 | convolution fusion | flops 1509949440 | bytes 25411584 | tf_op jit(solution)/shard_map/sgjd,ngd->sgjn/dot_general | solution.py:48
  147.6 55.4 %all-gather.7.cloned.1.call-done = bf16[6144,256]{1,0:T(8,128)(2,1)} async-done(((bf16[192,256]{1,0:T(8,128)(2,1)}), bf16[6144,256]{1,0:T(8,128)(2,1)}) %all-gather.7.cloned.1.call-update) | async-done | bytes 3145744 | tf_op jit(solution)/shard_map/all_gather | solution.py:57
  203.0 11.1 %fusion.3 = (f32[192,5]{0,1:T(8,128)S(1)}, f32[6144,192,5]{0,1,2:T(8,128)}) fusion(pred[192,6144]{1,0:T(8,128)(4,1)S(1)} %compare_and_fusion, bf16[192,5,128]{0,2,1:T(8,128)(2,1)S(1)} %bitcast.177, bf16[6144,256]{1,0:T(8,128)(2,1)} %all-gather.7.cloned.1.call-done), kind=kOutput, calls=%fused_computation.9 | convolution fusion | flops 1527643136 | bytes 26595072 | tf_op jit(solution)/shard_map/sgjd,ngd->sgjn/dot_general | solution.py:48
  214.1 11.4 %fusion.6 = f32[192,5]{0,1:T(8,128)S(1)} fusion(f32[6144,192,5]{0,1,2:T(8,128)} %get-tuple-element.28, f32[192,5]{0,1:T(8,128)S(1)} %broadcast_maximum_fusion, pred[192,6144]{1,0:T(8,128)(4,1)S(1)} %compare_and_fusion), kind=kLoop, calls=%fused_computation.12 | loop fusion | flops 23592000 | bytes 24780288 | tf_op jit(solution)/shard_map/reduce_sum | solution.py:74
  225.6 0.0 copy-start.9
  225.6 0.6 copy-done.9
  226.2 0.6 log_add_fusion
  226.8 13.2 %multiply_reduce_fusion = (f32[192,5]{0,1:T(8,128)}, bf16[192,1,5,128]{3,0,2,1:T(8,128)(2,1)S(1)}) fusion(f32[192,1,5,128]{3,0,2,1:T(8,128)S(1)} %copy.56, f32[192,5]{0,1:T(8,128)} %copy-done.9, f32[6144,192,5]{0,1,2:T(8,128)} %get-tuple-element.28, f32[192,5]{0,1:T(8,128)} %copy-done.10, pred[192,6144]{1,0:T(8,128)(4,1)S(1)} %compare_and_fusion, ...), kind=kOutput, calls=%fused_computation.51 | convolution fusion | flops 1534155776 | bytes 27102976 | tf_op jit(solution)/shard_map/sgjn,ngd->sgjd/dot_general | solution.py:68
  239.9 28.9 %all-gather.11.cloned.1.call-done = bf16[6144,128]{1,0:T(8,128)(2,1)} async-done(((bf16[192,128]{1,0:T(8,128)(2,1)}), bf16[6144,128]{1,0:T(8,128)(2,1)}) %all-gather.11.cloned.1.call-update) | async-done | bytes 1572880 | tf_op jit(solution)/shard_map/all_gather | solution.py:79
  268.9 15.8 %fusion.1 = bf16[192,1,5,6144]{3,0,2,1:T(8,128)(2,1)} fusion(f32[6144,192,5]{0,1,2:T(8,128)} %fusion.38, bf16[192,5,128]{0,2,1:T(8,128)(2,1)} %bitcast.181, f32[192,5]{0,1:T(8,128)} %get-tuple-element.29, f32[192,5]{0,1:T(8,128)} %log_add_fusion, pred[192,6144]{1,0:T(8,128)(4,1)S(1)} %compare_and_fusion, bf16[6144,128]{1,0:T(8,128)(2,1)} %all-gather.11.cloned.1.call-done), kind=kOutput, calls=%fused_computation.2 | convolution fusion | flops 1551237120 | bytes 38395392 | tf_op jit(solution)/shard_map/sgjd,ngd->sgjn/dot_general | solution.py:87
  284.6 9.9 %fusion.30 = bf16[6144,128]{1,0:T(8,128)(2,1)} fusion(bf16[192,5,128]{0,2,1:T(8,128)(2,1)S(1)} %bitcast.178, bf16[192,1,5,6144]{3,0,2,1:T(8,128)(2,1)} %fusion.1), kind=kOutput, calls=%fused_computation.28 | convolution fusion | flops 1510735872 | bytes 13615104 | tf_op jit(solution)/shard_map/sgjn,sgjd->ngd/dot_general | solution.py:98
  294.5 0.0 reduce-scatter.7.cloned.1.call-update
  294.5 0.0 reduce-scatter.9.cloned.1.call-start
  294.6 12.7 %fusion.27 = bf16[6144,128]{1,0:T(8,128)(2,1)} fusion(bf16[192,5,128]{0,2,1:T(8,128)(2,1)} %bitcast.182, f32[6144,192,5]{0,1,2:T(8,128)} %fusion.38, f32[192,5]{0,1:T(8,128)S(1)} %copy-done.12, pred[192,6144]{1,0:T(8,128)(4,1)} %copy-done.3), kind=kOutput, calls=%fused_computation.27 | convolution fusion | flops 1534328832 | bytes 26595072 | tf_op jit(solution)/shard_map/sgjn,sgjd->ngd/dot_general | solution.py:92
  307.4 0.0 reduce-scatter.9.cloned.1.call-update
  307.4 0.0 reduce-scatter.13.cloned.1.call-start
  307.4 100.8 %reduce-scatter.7.cloned.1.call-done = bf16[192,128]{1,0:T(8,128)(2,1)} async-done(((bf16[6144,128]{1,0:T(8,128)(2,1)}), bf16[192,128]{1,0:T(8,128)(2,1)}) %reduce-scatter.7.cloned.1.call-update) | async-done | bytes 49168 | tf_op jit(solution)/shard_map/reduce_scatter | solution.py:105
  408.2 120.1 %reduce-scatter.9.cloned.1.call-done = bf16[192,128]{1,0:T(8,128)(2,1)} async-done(((bf16[6144,128]{1,0:T(8,128)(2,1)}), bf16[192,128]{1,0:T(8,128)(2,1)}) %reduce-scatter.9.cloned.1.call-update) | async-done | bytes 49168 | tf_op jit(solution)/shard_map/reduce_scatter | solution.py:108
  528.3 0.0 copy-done.1
  528.3 3.2 fusion.34
  531.5 4.4 copy.69
  535.9 0.0 reduce-scatter.13.cloned.1.call-update
  535.9 0.0 reduce-scatter.11.cloned.1.call-start
  536.0 0.7 fusion.79
  536.6 0.0 copy-done.8
  536.7 3.4 fusion.33
  540.1 0.0 reduce-scatter.11.cloned.1.call-update
  540.1 0.2 copy.51
  540.3 0.9 copy.60
  541.2 6.1 fusion.48
  547.3 0.2 copy.57
  547.5 0.9 copy.61
  548.3 107.6 %reduce-scatter.13.cloned.1.call-done = bf16[160,256]{1,0:T(8,128)(2,1)} async-done(((bf16[5120,256]{1,0:T(8,128)(2,1)}), bf16[160,256]{1,0:T(8,128)(2,1)}) %reduce-scatter.13.cloned.1.call-update) | async-done | bytes 81936
  656.0 1.0 copy.70
  657.0 0.7 copy.62
  657.7 0.7 copy.63
  658.4 87.5 %reduce-scatter.11.cloned.1.call-done = bf16[24,5120]{1,0:T(8,128)(2,1)} async-done(((bf16[192,5120]{1,0:T(8,128)(2,1)}), bf16[24,5120]{1,0:T(8,128)(2,1)}) %reduce-scatter.11.cloned.1.call-update) | async-done | bytes 245776 | tf_op jit(solution)/shard_map/reduce_scatter | solution.py:114
  (23 shorter events, 0.1 us)
Async XLA Ops:
  7.2 63.6 %copy-start = (bf16[5120,128]{1,0:T(8,128)(2,1)S(1)}, bf16[5120,128]{1,0:T(8,128)(2,1)}, u32[]{:S(2)}) copy-start(bf16[5120,128]{1,0:T(8,128)(2,1)} %param.9) | copy-start | bytes 3932164
  7.2 70.7 %copy-start.4 = (bf16[192,640]{1,0:T(8,128)(2,1)S(1)}, bf16[192,640]{1,0:T(8,128)(2,1)}, u32[]{:S(2)}) copy-start(bf16[192,640]{1,0:T(8,128)(2,1)} %param.11) | copy-start | bytes 737284
  7.2 63.6 %all-gather.5.cloned.1.call-start = ((), (), s32[]{:S(2)}) async-start(), calls=%async_computation.4 | async-start | bytes 2211840 | tf_op jit(solution)/shard_map/all_gather | solution.py:15
  7.9 127.2 %all-gather.9.cloned.1.call-start = ((), (), s32[]{:S(2)}) async-start(), calls=%async_computation.6 | async-start | bytes 1622016 | tf_op jit(solution)/shard_map/all_gather | solution.py:78
  73.6 5.7 copy-start.13
  73.6 6.1 copy-start.11
  73.6 6.2 copy-start.6
  73.6 129.4 %all-gather.7.cloned.1.call-start = ((), (), s32[]{:S(2)}) async-start(), calls=%async_computation.5 | async-start | bytes 3244032 | tf_op jit(solution)/shard_map/all_gather | solution.py:57
  76.3 4.6 copy-start.5
  77.8 191.0 %all-gather.11.cloned.1.call-start = ((), (), s32[]{:S(2)}) async-start(), calls=%async_computation.7 | async-start | bytes 1622016 | tf_op jit(solution)/shard_map/all_gather | solution.py:79
  81.0 187.9 %copy-start.3 = (pred[192,6144]{1,0:T(8,128)(4,1)}, pred[192,6144]{1,0:T(8,128)(4,1)S(1)}, u32[]{:S(2)}) copy-start(pred[192,6144]{1,0:T(8,128)(4,1)S(1)} %compare_and_fusion) | copy-start | bytes 3538948
  81.0 327.2 %reduce-scatter.7.cloned.1.call-start = ((), (), s32[]{:S(2)}) async-start(), calls=%async_computation.8 | async-start | bytes 1622016 | tf_op jit(solution)/shard_map/reduce_scatter | solution.py:105
  214.1 11.4 %copy-start.10 = (f32[192,5]{0,1:T(8,128)}, f32[192,5]{0,1:T(8,128)S(1)}, u32[]{:S(2)}) copy-start(f32[192,5]{0,1:T(8,128)S(1)} %broadcast_maximum_fusion) | copy-start | bytes 11524
  225.6 0.6 copy-start.9
  284.6 10.0 %copy-start.12 = (f32[192,5]{0,1:T(8,128)S(1)}, f32[192,5]{0,1:T(8,128)}, u32[]{:S(2)}) copy-start(f32[192,5]{0,1:T(8,128)} %log_add_fusion) | copy-start | bytes 11524
  294.5 233.7 %copy-start.1 = (bf16[192,5120]{1,0:T(8,128)(2,1)S(1)}, bf16[192,5120]{1,0:T(8,128)(2,1)}, u32[]{:S(2)}) copy-start(bf16[192,5120]{1,0:T(8,128)(2,1)} %all-gather.5.cloned.1.call-done) | copy-start | bytes 5898244
  294.5 233.7 %reduce-scatter.9.cloned.1.call-start = ((), (), s32[]{:S(2)}) async-start(), calls=%async_computation.9 | async-start | bytes 1622016 | tf_op jit(solution)/shard_map/reduce_scatter | solution.py:108
  307.4 348.6 %reduce-scatter.13.cloned.1.call-start = ((), (), s32[]{:S(2)}) async-start(), calls=%async_computation.11 | async-start | bytes 2703360
  531.5 4.5 copy-start.7
  535.9 0.8 copy-start.8
  535.9 210.1 %reduce-scatter.11.cloned.1.call-start = ((), (), s32[]{:S(2)}) async-start(), calls=%async_computation.10 | async-start | bytes 2211840 | tf_op jit(solution)/shard_map/reduce_scatter | solution.py:114
  536.7 4.5 copy-start.2
Sparse Core Ops, SparseCore 0:
  10.6 60.1 all-gather.4
  73.8 61.2 all-gather.8
  137.6 65.4 all-gather.6
  205.3 63.5 all-gather.10
  294.7 113.4 reduce-scatter.6
  410.5 117.6 reduce-scatter.8
  536.0 119.8 reduce-scatter.12
  660.6 85.3 reduce-scatter.10
